TPU v7x, 32 devices: a whole 2x2x4 slice. The times are simulated.
32 devices in a mesh: dp: 2 (over x), expert: 16 (over z, y, core).
Axes of the slice: x: 2, y: 2, z: 4, core: 2. Of those that a mesh axis runs over, the one named last changes fastest.
Arguments:
- tokens: bfloat16 [4096, 1792], P(('dp', 'expert')), may hold values from -6 to 6
- routes: int32 [4096, 4], P(('dp', 'expert')), may hold values from 0 to 15, all different within a row; in each aligned block of 128 rows (0 to 127, 128 to 255, ...) at most 64 rows name the same one
- route_weight: float32 [4096, 4], P(('dp', 'expert')), may hold values from 0.1 to 1
- w_in: float32 [16, 2, 1792, 1280], P('expert', None, 'dp'), may hold values from -0.125 to 0.125
- m_in: float32 [16, 2, 1792, 1280], P('expert', None, 'dp'), may hold values from -6 to 6
- v_in: float32 [16, 2, 1792, 1280], P('expert', None, 'dp'), may hold values from 0.5 to 20
- g_in: bfloat16 [16, 2, 1792, 1280], P('expert', None, 'dp'), may hold values from -30 to 30
- w_out: float32 [16, 1280, 1792], P('expert', 'dp'), may hold values from -0.15625 to 0.15625
- m_out: float32 [16, 1280, 1792], P('expert', 'dp'), may hold values from -6 to 6
- v_out: float32 [16, 1280, 1792], P('expert', 'dp'), may hold values from 0.5 to 20
- g_out: bfloat16 [16, 1280, 1792], P('expert', 'dp'), may hold values from -30 to 30
Outputs:
- mixed: bfloat16 [4096, 1792], P(('dp', 'expert'))
Inputs may be any that keep to these rules, and one draw needn't show every extreme that they name: `routes`: A token's 4 experts differ. Within the rows of one device (aligned blocks of 128 tokens) each expert is named at most 64 times, a bound that some block reaches.
All inputs are finite; a program needn't handle non-finite values.
Results may differ from a plain program's by a relative error of at most 0.008.
Values may be sent and summed in bfloat16 or wider, within the bound.
No kernel may reach another device: no remote copies, remote signals or barrier semaphores. Data moves between devices by JAX's collectives and lax.ppermute only.
A program may use at most 128 MiB of HBM per device.

v0:
```python
import jax
import jax.numpy as jnp
from jax import lax
from jax.sharding import PartitionSpec as P

beta_one = 0.9
beta_two = 0.95
corr_one = 0.99997343860111
corr_two = 0.99407947077967
adam_eps = 1e-08
learn_rate = 0.01
weight_decay = 0.1


def adamw(master, moment, second, gradient):
    grad_value = gradient.astype(jnp.float32)
    moment_new = beta_one * moment + (1.0 - beta_one) * grad_value
    second_new = beta_two * second + (1.0 - beta_two) * grad_value * grad_value
    update = moment_new / corr_one / (jnp.sqrt(second_new / corr_two) + adam_eps)
    return (master - learn_rate * (update + weight_decay * master)).astype(jnp.bfloat16)


def expert_apply(block_rows, gate_up, down_proj):
    gate_pre = jnp.dot(block_rows, gate_up[0], preferred_element_type=jnp.float32)
    up_pre = jnp.dot(block_rows, gate_up[1], preferred_element_type=jnp.float32)
    hidden = (jax.nn.silu(gate_pre) * up_pre).astype(jnp.bfloat16)
    return jnp.dot(hidden, down_proj, preferred_element_type=jnp.float32).astype(jnp.bfloat16)


def per_device(tokens, routes, route_weight, w_in, m_in, v_in, g_in, w_out, m_out, v_out, g_out):
    groups = lax.axis_size("expert")
    tok_rows, width = tokens.shape
    top_count = routes.shape[1]
    capacity = 2 * tok_rows * top_count // groups
    slot_total = groups * capacity
    flat_routes = routes.reshape(-1)
    owners = jnp.arange(tok_rows * top_count, dtype=jnp.int32) // top_count
    onehot = (flat_routes[:, None] == jnp.arange(groups, dtype=jnp.int32)[None, :]).astype(
        jnp.int32
    )
    earlier = jnp.cumsum(onehot, axis=0) - onehot
    slot_ids = flat_routes * capacity + jnp.sum(earlier * onehot, axis=1)
    matches = (jnp.arange(slot_total, dtype=jnp.int32)[:, None] == slot_ids[None, :]).astype(
        jnp.int32
    )
    live_flags = jnp.sum(matches, axis=1)
    sources = jnp.sum(matches * owners[None, :], axis=1)
    outgoing = jnp.where(
        live_flags[:, None] > 0, jnp.take(tokens, sources, axis=0), jnp.zeros((), jnp.bfloat16)
    )
    outgoing = outgoing.reshape(groups, capacity, width)
    gate_up_own = adamw(w_in, m_in, v_in, g_in)
    down_own = adamw(w_out, m_out, v_out, g_out)
    gate_up_all, down_all = (
        lax.all_gather(gate_up_own, "dp", axis=2, tiled=True),
        lax.all_gather(down_own, "dp", axis=1, tiled=True),
    )
    gate_up_all = gate_up_all[0]
    down_all = down_all[0]
    arrived = lax.all_to_all(outgoing, "expert", split_axis=0, concat_axis=0, tiled=True)
    src_count, item_count, depth = arrived.shape
    results = expert_apply(arrived.reshape(src_count * item_count, depth), gate_up_all, down_all)
    returned = lax.all_to_all(
        results.reshape(src_count, item_count, depth),
        "expert",
        split_axis=0,
        concat_axis=0,
        tiled=True,
    )
    back_rows = returned.reshape(slot_total, width)
    picked = jnp.take(back_rows, slot_ids, axis=0).reshape(tok_rows, top_count, width)
    mixed = jnp.einsum("tkd,tk->td", picked.astype(jnp.float32), route_weight)
    return mixed.astype(jnp.bfloat16)


def solution(mesh):
    placed = (
        P(("dp", "expert"), None),
        P(("dp", "expert"), None),
        P(("dp", "expert"), None),
        P("expert", None, "dp", None),
        P("expert", None, "dp", None),
        P("expert", None, "dp", None),
        P("expert", None, "dp", None),
        P("expert", "dp", None),
        P("expert", "dp", None),
        P("expert", "dp", None),
        P("expert", "dp", None),
    )
    return jax.shard_map(
        per_device, mesh=mesh, in_specs=placed, out_specs=P(("dp", "expert"), None), check_vma=False
    )
```

profile of v0, /device:TPU:13, one launch (start us, length us, event | category | flops | bytes accessed | tf_op | source)
XLA Modules:
  0.0 321.8 jit_solution(14130354213369942795)
XLA Ops:
  6.5 15.8 %fusion.10 = bf16[1,2,896,1280]{3,2,1,0:T(8,128)(2,1)} fusion(f32[1,2,896,1280]{3,2,1,0:T(8,128)} %param.14, f32[1,2,896,1280]{3,2,1,0:T(8,128)} %param.16, bf16[1,2,896,1280]{3,2,1,0:T(8,128)(2,1)} %param.17, f32[1,2,896,1280]{3,2,1,0:T(8,128)} %param.15), kind=kLoop, calls=%fused_computation.14 | loop fusion | flops 38993920 | bytes 36700160 | tf_op jit(solution)/shard_map/convert_element_type | solution.py:20
  22.4 0.7 copy-done.3
  23.1 0.1 copy.21
  23.2 0.1 eq.39
  23.3 0.1 reshape.133
  23.4 1.2 reduce-window.6
  24.6 0.2 slice_reduce_fusion
  24.8 0.1 fusion.34
  24.9 0.6 convert_reduce_fusion
  25.6 0.1 reduce_sum.39
  25.6 0.1 gt.20
  25.8 5.8 %gather_fusion = bf16[1024,1792]{1,0:T(8,128)(2,1)} fusion(bf16[128,1792]{1,0:T(8,128)(2,1)S(1)} %copy-done, s32[1024]{0:T(1024)S(1)} %broadcast_clamp_fusion), kind=kCustom, calls=%fused_computation | custom fusion | bytes 7344128 | tf_op jit(solution)/shard_map/jit(_take)/gather | solution.py:49
  31.6 4.7 %select_select_fusion = bf16[16,64,1792]{2,1,0:T(8,128)(2,1)} fusion(bf16[16,64,1792]{2,1,0:T(8,128)(2,1)} %bitcast.47, pred[16,64]{1,0:T(8,128)(4,1)S(1)} %compare_and_fusion, pred[16,64]{1,0:T(8,128)(4,1)S(1)} %gt.20), kind=kLoop, calls=%fused_computation.35 | loop fusion | flops 3670016 | bytes 7342080 | tf_op jit(solution)/shard_map/jit(_where)/select_n | solution.py:48
  36.3 6.7 %all-to-all-start = ((bf16[16,64,1792]{2,1,0:T(8,128)(2,1)}), bf16[16,64,1792]{2,1,0:T(8,128)(2,1)}, u32[]{:S(2)}, u32[]{:S(2)}) async-start(bf16[16,64,1792]{2,1,0:T(8,128)(2,1)} %select_select_fusion), calls=%async_computation | async-start | bytes 7340032 | tf_op jit(solution)/shard_map/all_to_all | solution.py:60
  43.1 0.2 all-gather.5.cloned.1.call-start
  43.3 7.9 %fusion.24 = bf16[1,640,1792]{2,1,0:T(8,128)(2,1)} fusion(f32[1,640,1792]{2,1,0:T(8,128)} %param.18, f32[1,640,1792]{2,1,0:T(8,128)} %param.20, bf16[1,640,1792]{2,1,0:T(8,128)(2,1)S(1)} %copy-done.2, f32[1,640,1792]{2,1,0:T(8,128)} %param.19), kind=kLoop, calls=%fused_computation.33 | loop fusion | flops 19496960 | bytes 18350080 | tf_op jit(solution)/shard_map/convert_element_type | solution.py:20
  51.3 73.3 %all-to-all-done = bf16[16,64,1792]{2,1,0:T(8,128)(2,1)} async-done(((bf16[16,64,1792]{2,1,0:T(8,128)(2,1)}), bf16[16,64,1792]{2,1,0:T(8,128)(2,1)}, u32[]{:S(2)}, u32[]{:S(2)}) %all-to-all-start) | async-done | bytes 3670048 | tf_op jit(solution)/shard_map/all_to_all | solution.py:60
  124.6 12.0 %all-gather.3.cloned.1.call-done = bf16[1,2,1792,1280]{3,2,1,0:T(8,128)(2,1)} async-done(((bf16[1,2,896,1280]{3,2,1,0:T(8,128)(2,1)}), bf16[1,2,1792,1280]{3,2,1,0:T(8,128)(2,1)}) %all-gather.3.cloned.1.call-update) | async-done | bytes 9175056 | tf_op jit(solution)/shard_map/all_gather | solution.py:55
  136.5 11.0 %fusion.21 = f32[1024,1280]{1,0:T(8,128)} fusion(bf16[1024,1792]{1,0:T(8,128)(2,1)} %bitcast.4, bf16[1,2,1792,1280]{3,2,1,0:T(8,128)(2,1)} %all-gather.3.cloned.1.call-done), kind=kOutput, calls=%fused_computation.30 | convolution fusion | flops 4697620480 | bytes 13500416 | tf_op jit(solution)/shard_map/dot_general | solution.py:24
  147.5 51.8 %all-gather.5.cloned.1.call-done = bf16[1,1280,1792]{2,1,0:T(8,128)(2,1)} async-done(((bf16[1,640,1792]{2,1,0:T(8,128)(2,1)}), bf16[1,1280,1792]{2,1,0:T(8,128)(2,1)}) %all-gather.5.cloned.1.call-update) | async-done | bytes 4587536 | tf_op jit(solution)/shard_map/all_gather | solution.py:56
  199.3 16.4 %fusion.25 = bf16[1024,1792]{1,0:T(8,128)(2,1)} fusion(bf16[1,1280,1792]{2,1,0:T(8,128)(2,1)} %all-gather.5.cloned.1.call-done, f32[1024,1280]{1,0:T(8,128)} %fusion.21, bf16[1024,1792]{1,0:T(8,128)(2,1)} %bitcast.4, bf16[1,2,1792,1280]{3,2,1,0:T(8,128)(2,1)} %all-gather.3.cloned.1.call-done), kind=kOutput, calls=%fused_computation.34 | convolution fusion | flops 9404940288 | bytes 21757952 | tf_op jit(solution)/shard_map/dot_general | solution.py:27
  215.6 6.6 %all-to-all-start.1 = ((bf16[16,64,1792]{2,1,0:T(8,128)(2,1)}), bf16[16,64,1792]{2,1,0:T(8,128)(2,1)}, u32[]{:S(2)}, u32[]{:S(2)}) async-start(bf16[16,64,1792]{2,1,0:T(8,128)(2,1)} %bitcast.48), calls=%async_computation.1 | async-start | bytes 7340032 | tf_op jit(solution)/shard_map/all_to_all | solution.py:63
  222.3 0.1 reduce_sum.36
  222.4 0.1 copy.26
  222.5 0.1 mul.142
  222.7 0.1 copy.25
  222.9 0.2 copy.27
  223.1 80.5 %all-to-all-done.1 = bf16[16,64,1792]{2,1,0:T(8,128)(2,1)} async-done(((bf16[16,64,1792]{2,1,0:T(8,128)(2,1)}), bf16[16,64,1792]{2,1,0:T(8,128)(2,1)}, u32[]{:S(2)}, u32[]{:S(2)}) %all-to-all-start.1) | async-done | bytes 3670048 | tf_op jit(solution)/shard_map/all_to_all | solution.py:63
  303.5 6.5 %gather_fusion.1 = bf16[512,1792]{1,0:T(8,128)(2,1)S(1)} fusion(bf16[1024,1792]{1,0:T(8,128)(2,1)} %bitcast.9, s32[1024]{0:T(1024)S(1)} %pad_clamp_fusion), kind=kCustom, calls=%fused_computation.1 | custom fusion | bytes 3672064 | tf_op jit(solution)/shard_map/jit(_take)/gather | solution.py:71
  310.0 1.5 gather.15
  311.5 2.7 fusion.28
  314.2 0.8 copy.32
  (25 shorter events, 0.2 us)
Async XLA Ops:
  6.5 19.2 %copy-start = (bf16[128,1792]{1,0:T(8,128)(2,1)S(1)}, bf16[128,1792]{1,0:T(8,128)(2,1)}, u32[]{:S(2)}) copy-start(bf16[128,1792]{1,0:T(8,128)(2,1)} %param.11) | copy-start | bytes 1376260
  6.5 130.0 %all-gather.3.cloned.1.call-start = ((), (), s32[]{:S(2)}) async-start(), calls=%async_computation.2 | async-start | bytes 13762560 | tf_op jit(solution)/shard_map/all_gather | solution.py:55
  22.4 0.7 copy-start.3
  36.3 7.0 %copy-start.2 = (bf16[1,640,1792]{2,1,0:T(8,128)(2,1)S(1)}, bf16[1,640,1792]{2,1,0:T(8,128)(2,1)}, u32[]{:S(2)}) copy-start(bf16[1,640,1792]{2,1,0:T(8,128)(2,1)} %param.21) | copy-start | bytes 6881284
  36.3 88.3 %all-to-all-start = ((bf16[16,64,1792]{2,1,0:T(8,128)(2,1)}), bf16[16,64,1792]{2,1,0:T(8,128)(2,1)}, u32[]{:S(2)}, u32[]{:S(2)}) async-start(bf16[16,64,1792]{2,1,0:T(8,128)(2,1)} %select_select_fusion), calls=%async_computation | async-start | bytes 7340032 | tf_op jit(solution)/shard_map/all_to_all | solution.py:60
  43.1 156.2 %all-gather.5.cloned.1.call-start = ((), (), s32[]{:S(2)}) async-start(), calls=%async_computation.3 | async-start | bytes 6881280 | tf_op jit(solution)/shard_map/all_gather | solution.py:56
  215.6 7.2 %copy-start.4 = (f32[128,4]{0,1:T(4,128)S(1)}, f32[128,4]{0,1:T(4,128)}, u32[]{:S(2)}) copy-start(f32[128,4]{0,1:T(4,128)} %param.13) | copy-start | bytes 6148
  215.6 87.9 %all-to-all-start.1 = ((bf16[16,64,1792]{2,1,0:T(8,128)(2,1)}), bf16[16,64,1792]{2,1,0:T(8,128)(2,1)}, u32[]{:S(2)}, u32[]{:S(2)}) async-start(bf16[16,64,1792]{2,1,0:T(8,128)(2,1)} %bitcast.48), calls=%async_computation.1 | async-start | bytes 7340032 | tf_op jit(solution)/shard_map/all_to_all | solution.py:63
  310.0 5.0 %copy-start.1 = (bf16[128,1792]{1,0:T(8,128)(2,1)S(1)}, bf16[128,1792]{1,0:T(8,128)(2,1)}, u32[]{:S(2)}) copy-start(bf16[128,1792]{1,0:T(8,128)(2,1)} %param.11) | copy-start | bytes 1376260
Sparse Core Ops, SparseCore 0:
  22.5 113.9 all-gather.2
  138.1 61.1 all-gather.4
where the time goes:
time: 322 us
  waiting for transfers between devices  218 us (68%)
  other arithmetic  30.5 us (9%)
  matrix products  30 us (9%)
  local copies, waits for them, and re-layouts  16.6 us (5%)
  starting transfers between devices  13.6 us (4%)
  between operations  13.5 us (4%)
    all_to_all x1, waiting for transfers between devices, per_device(): lax.all_to_all(results.reshape(src_count, item_count, depth), 'expert', s...  80.5 us
    all_to_all x1, waiting for transfers between devices, per_device(): lax.all_to_all(outgoing, 'expert', split_axis=0, concat_axis=0, tiled=True)  73.3 us
    all_gather x1, waiting for transfers between devices, per_device(): lax.all_gather(down_own, 'dp', axis=1, tiled=True)  51.8 us
    convert_element_type x2, other arithmetic, adamw(): (master - learn_rate * (update + weight_decay * master)).astype(jnp.bfloa...  23.8 us
    dot_general x1, matrix products, expert_apply(): jnp.dot(hidden, down_proj, preferred_element_type=jnp.float32)  16.4 us
    all_gather x1, waiting for transfers between devices, per_device(): lax.all_gather(gate_up_own, 'dp', axis=2, tiled=True)  12 us
    dot_general x1, matrix products, expert_apply(): jnp.dot(block_rows, gate_up[0], preferred_element_type=jnp.float32)  11 us
    gather x2, local copies, waits for them, and re-layouts, per_device(): jnp.take(back_rows, slot_ids, axis=0).reshape(tok_rows, top_count, width)  7.94 us
  transfers between devices with their start and end apart: 4, of which 4 were waited for; matrix products, arithmetic and copies ran while one was open for 10% of the time, Pallas kernels for 0%

commit v1 on v0

--- a/solution.py
+++ b/solution.py
@@ -53,7 +53,9 @@
     down_own = adamw(w_out, m_out, v_out, g_out)
     gate_up_all, down_all = (
         lax.all_gather(gate_up_own, "dp", axis=2, tiled=True),
-        lax.all_gather(down_own, "dp", axis=1, tiled=True),
+        jnp.concatenate(
+            lax.all_to_all(jnp.stack([down_own] * lax.axis_size("dp")), "dp", 0, 0), axis=1
+        ),
     )
     gate_up_all = gate_up_all[0]
     down_all = down_all[0]

time: 322 us -> 308 us (0.957)
  waiting for transfers between devices: 218 us -> 197 us
  starting transfers between devices: 13.6 us -> 18.9 us
    all_gather x1 -> x0, waiting for transfers between devices: 51.8 us -> none  [per_device(): lax.all_gather(down_own, 'dp', axis=1, tiled=True)]
    all_to_all x0 -> x1, waiting for transfers between devices: none -> 35.6 us  [per_device(): lax.all_to_all(jnp.stack([down_own] * lax.axis_size('dp')), 'dp', 0, 0)]
    another operation x2 -> x4, other arithmetic: 1.19 us -> 10.7 us  [the longest x2 9.51 us: per_device(): jnp.stack([down_own] * lax.axis_size('dp'))]
    convert_element_type x2 -> x1, other arithmetic: 23.8 us -> 15.8 us  [adamw(): (master - learn_rate * (update + weight_decay * master)).astype(jnp.bfloa...]
    all_to_all x0 -> x1, starting transfers between devices: none -> 5.91 us  [per_device(): lax.all_to_all(jnp.stack([down_own] * lax.axis_size('dp')), 'dp', 0, 0)]
  transfers between devices with their start and end apart: 4 -> 4, of which waited for: 4 -> 4; matrix products, arithmetic and copies ran while one was open for 10% -> 11% of each run, Pallas kernels for 0% -> 0%
where the time goes in v1:
time: 308 us
  waiting for transfers between devices  197 us (64%)
  other arithmetic  32 us (10%)
  matrix products  29.7 us (10%)
  starting transfers between devices  18.9 us (6%)
  local copies, waits for them, and re-layouts  16.6 us (5%)
  between operations  13.5 us (4%)
    all_to_all x1, waiting for transfers between devices, per_device(): lax.all_to_all(results.reshape(src_count, item_count, depth), 'expert', s...  80.5 us
    all_to_all x1, waiting for transfers between devices, per_device(): lax.all_to_all(outgoing, 'expert', split_axis=0, concat_axis=0, tiled=True)  72 us
    all_to_all x1, waiting for transfers between devices, per_device(): lax.all_to_all(jnp.stack([down_own] * lax.axis_size('dp')), 'dp', 0, 0)  35.6 us
    dot_general x1, matrix products, expert_apply(): jnp.dot(hidden, down_proj, preferred_element_type=jnp.float32)  16.3 us
    convert_element_type x1, other arithmetic, adamw(): (master - learn_rate * (update + weight_decay * master)).astype(jnp.bfloa...  15.8 us
    dot_general x1, matrix products, expert_apply(): jnp.dot(block_rows, gate_up[0], preferred_element_type=jnp.float32)  10.7 us
    another operation x2, other arithmetic, per_device(): jnp.stack([down_own] * lax.axis_size('dp'))  9.51 us
    all_gather x1, waiting for transfers between devices, per_device(): lax.all_gather(gate_up_own, 'dp', axis=2, tiled=True)  9.25 us
  transfers between devices with their start and end apart: 4, of which 4 were waited for; matrix products, arithmetic and copies ran while one was open for 11% of the time, Pallas kernels for 0%

profile of v1, /device:TPU:13, one launch (start us, length us, event | category | flops | bytes accessed | tf_op | source)
XLA Modules:
  0.0 308.1 jit_solution(387371071810607816)
XLA Ops:
  6.5 15.8 %fusion.10 = bf16[1,2,896,1280]{3,2,1,0:T(8,128)(2,1)} fusion(f32[1,2,896,1280]{3,2,1,0:T(8,128)} %param.14, f32[1,2,896,1280]{3,2,1,0:T(8,128)} %param.16, bf16[1,2,896,1280]{3,2,1,0:T(8,128)(2,1)} %param.17, f32[1,2,896,1280]{3,2,1,0:T(8,128)} %param.15), kind=kLoop, calls=%fused_computation.14 | loop fusion | flops 38993920 | bytes 36700160 | tf_op jit(solution)/shard_map/convert_element_type | solution.py:20
  22.4 0.7 copy-done.3
  23.1 0.1 copy.21
  23.2 0.1 reshape.133
  23.3 0.1 eq.39
  23.4 1.2 reduce-window.6
  24.6 0.2 slice_reduce_fusion
  24.8 0.1 fusion.30
  24.9 0.6 convert_reduce_fusion
  25.7 0.1 gt.20
  25.8 5.8 %gather_fusion = bf16[1024,1792]{1,0:T(8,128)(2,1)} fusion(bf16[128,1792]{1,0:T(8,128)(2,1)S(1)} %copy-done, s32[1024]{0:T(1024)S(1)} %broadcast_clamp_fusion), kind=kCustom, calls=%fused_computation | custom fusion | bytes 7344128 | tf_op jit(solution)/shard_map/jit(_take)/gather | solution.py:49
  31.6 4.6 %select_select_fusion = bf16[16,64,1792]{2,1,0:T(8,128)(2,1)} fusion(bf16[16,64,1792]{2,1,0:T(8,128)(2,1)} %bitcast.53, pred[16,64]{1,0:T(8,128)(4,1)S(1)} %compare_and_fusion, pred[16,64]{1,0:T(8,128)(4,1)S(1)} %gt.20), kind=kLoop, calls=%fused_computation.34 | loop fusion | flops 3670016 | bytes 7342080 | tf_op jit(solution)/shard_map/jit(_where)/select_n | solution.py:48
  36.2 6.7 %all-to-all-start = ((bf16[16,64,1792]{2,1,0:T(8,128)(2,1)}), bf16[16,64,1792]{2,1,0:T(8,128)(2,1)}, u32[]{:S(2)}, u32[]{:S(2)}) async-start(bf16[16,64,1792]{2,1,0:T(8,128)(2,1)} %select_select_fusion), calls=%async_computation | async-start | bytes 7340032 | tf_op jit(solution)/shard_map/all_to_all | solution.py:62
  43.0 7.0 %fusion.23 = bf16[1,1,640,1792]{3,2,1,0:T(8,128)(2,1)S(1)} fusion(f32[1,640,1792]{2,1,0:T(8,128)} %param.18, f32[1,640,1792]{2,1,0:T(8,128)} %param.20, bf16[1,640,1792]{2,1,0:T(8,128)(2,1)S(1)} %copy-done.2, f32[1,640,1792]{2,1,0:T(8,128)} %param.19), kind=kLoop, calls=%fused_computation.35 | loop fusion | flops 19496960 | bytes 18350080 | tf_op jit(solution)/shard_map/stack | solution.py:57
  50.0 2.5 pad_maximum_fusion
  52.5 72.0 %all-to-all-done = bf16[16,64,1792]{2,1,0:T(8,128)(2,1)} async-done(((bf16[16,64,1792]{2,1,0:T(8,128)(2,1)}), bf16[16,64,1792]{2,1,0:T(8,128)(2,1)}, u32[]{:S(2)}, u32[]{:S(2)}) %all-to-all-start) | async-done | bytes 3670048 | tf_op jit(solution)/shard_map/all_to_all | solution.py:62
  124.5 5.9 %all-to-all-start.1 = ((bf16[2,1,640,1792]{3,2,1,0:T(8,128)(2,1)}), bf16[2,1,640,1792]{3,2,1,0:T(8,128)(2,1)}, u32[]{:S(2)}, u32[]{:S(2)}) async-start(bf16[2,1,640,1792]{3,2,1,0:T(8,128)(2,1)} %pad_maximum_fusion), calls=%async_computation.1 | async-start | bytes 9175040 | tf_op jit(solution)/shard_map/all_to_all | solution.py:57
  130.4 9.2 %all-gather.2.cloned.1.call-done = bf16[1,2,1792,1280]{3,2,1,0:T(8,128)(2,1)} async-done(((bf16[1,2,896,1280]{3,2,1,0:T(8,128)(2,1)}), bf16[1,2,1792,1280]{3,2,1,0:T(8,128)(2,1)}) %all-gather.2.cloned.1.call-update) | async-done | bytes 9175056 | tf_op jit(solution)/shard_map/all_gather | solution.py:55
  139.6 10.7 %fusion.21 = f32[1024,1280]{1,0:T(8,128)} fusion(bf16[1024,1792]{1,0:T(8,128)(2,1)} %bitcast.4, bf16[1,2,1792,1280]{3,2,1,0:T(8,128)(2,1)} %all-gather.2.cloned.1.call-done), kind=kOutput, calls=%fused_computation.30 | convolution fusion | flops 4697620480 | bytes 13500416 | tf_op jit(solution)/shard_map/dot_general | solution.py:24
  150.3 35.6 %all-to-all-done.1 = bf16[2,1,640,1792]{3,2,1,0:T(8,128)(2,1)} async-done(((bf16[2,1,640,1792]{3,2,1,0:T(8,128)(2,1)}), bf16[2,1,640,1792]{3,2,1,0:T(8,128)(2,1)}, u32[]{:S(2)}, u32[]{:S(2)}) %all-to-all-start.1) | async-done | bytes 4587552 | tf_op jit(solution)/shard_map/all_to_all | solution.py:57
  185.9 16.3 %convolution_convert_fusion = bf16[1024,1792]{1,0:T(8,128)(2,1)} fusion(bf16[1280,1792]{1,0:T(8,128)(2,1)} %bitcast.8, f32[1024,1280]{1,0:T(8,128)} %fusion.21, bf16[1024,1792]{1,0:T(8,128)(2,1)} %bitcast.4, bf16[1,2,1792,1280]{3,2,1,0:T(8,128)(2,1)} %all-gather.2.cloned.1.call-done), kind=kOutput, calls=%fused_computation.33 | convolution fusion | flops 9404940288 | bytes 21757952 | tf_op jit(solution)/shard_map/dot_general | solution.py:27
  202.3 6.2 %all-to-all-start.2 = ((bf16[16,64,1792]{2,1,0:T(8,128)(2,1)}), bf16[16,64,1792]{2,1,0:T(8,128)(2,1)}, u32[]{:S(2)}, u32[]{:S(2)}) async-start(bf16[16,64,1792]{2,1,0:T(8,128)(2,1)} %bitcast.54), calls=%async_computation.2 | async-start | bytes 7340032 | tf_op jit(solution)/shard_map/all_to_all | solution.py:65
  208.5 0.1 reduce_sum.36
  208.6 0.2 copy.27
  208.8 0.1 copy.26
  208.9 0.1 mul.142
  209.1 0.1 copy.25
  209.3 80.5 %all-to-all-done.2 = bf16[16,64,1792]{2,1,0:T(8,128)(2,1)} async-done(((bf16[16,64,1792]{2,1,0:T(8,128)(2,1)}), bf16[16,64,1792]{2,1,0:T(8,128)(2,1)}, u32[]{:S(2)}, u32[]{:S(2)}) %all-to-all-start.2) | async-done | bytes 3670048 | tf_op jit(solution)/shard_map/all_to_all | solution.py:65
  289.7 6.5 %gather_fusion.1 = bf16[512,1792]{1,0:T(8,128)(2,1)S(1)} fusion(bf16[1024,1792]{1,0:T(8,128)(2,1)} %bitcast.10, s32[1024]{0:T(1024)S(1)} %pad_clamp_fusion), kind=kCustom, calls=%fused_computation.1 | custom fusion | bytes 3672064 | tf_op jit(solution)/shard_map/jit(_take)/gather | solution.py:73
  296.2 1.5 gather.15
  297.7 2.7 fusion.24
  300.4 0.8 copy.32
  (25 shorter events, 0.3 us)
Async XLA Ops:
  6.5 19.2 %copy-start = (bf16[128,1792]{1,0:T(8,128)(2,1)S(1)}, bf16[128,1792]{1,0:T(8,128)(2,1)}, u32[]{:S(2)}) copy-start(bf16[128,1792]{1,0:T(8,128)(2,1)} %param.11) | copy-start | bytes 1376260
  6.5 133.1 %all-gather.2.cloned.1.call-start = ((), (), s32[]{:S(2)}) async-start(), calls=%async_computation.3 | async-start | bytes 13762560 | tf_op jit(solution)/shard_map/all_gather | solution.py:55
  22.4 0.7 copy-start.3
  36.2 6.7 %copy-start.2 = (bf16[1,640,1792]{2,1,0:T(8,128)(2,1)S(1)}, bf16[1,640,1792]{2,1,0:T(8,128)(2,1)}, u32[]{:S(2)}) copy-start(bf16[1,640,1792]{2,1,0:T(8,128)(2,1)} %param.21) | copy-start | bytes 6881284
  36.2 88.3 %all-to-all-start = ((bf16[16,64,1792]{2,1,0:T(8,128)(2,1)}), bf16[16,64,1792]{2,1,0:T(8,128)(2,1)}, u32[]{:S(2)}, u32[]{:S(2)}) async-start(bf16[16,64,1792]{2,1,0:T(8,128)(2,1)} %select_select_fusion), calls=%async_computation | async-start | bytes 7340032 | tf_op jit(solution)/shard_map/all_to_all | solution.py:62
  124.5 61.5 %all-to-all-start.1 = ((bf16[2,1,640,1792]{3,2,1,0:T(8,128)(2,1)}), bf16[2,1,640,1792]{3,2,1,0:T(8,128)(2,1)}, u32[]{:S(2)}, u32[]{:S(2)}) async-start(bf16[2,1,640,1792]{3,2,1,0:T(8,128)(2,1)} %pad_maximum_fusion), calls=%async_computation.1 | async-start | bytes 9175040 | tf_op jit(solution)/shard_map/all_to_all | solution.py:57
  202.3 6.4 %copy-start.4 = (f32[128,4]{0,1:T(4,128)S(1)}, f32[128,4]{0,1:T(4,128)}, u32[]{:S(2)}) copy-start(f32[128,4]{0,1:T(4,128)} %param.13) | copy-start | bytes 6148
  202.3 87.5 %all-to-all-start.2 = ((bf16[16,64,1792]{2,1,0:T(8,128)(2,1)}), bf16[16,64,1792]{2,1,0:T(8,128)(2,1)}, u32[]{:S(2)}, u32[]{:S(2)}) async-start(bf16[16,64,1792]{2,1,0:T(8,128)(2,1)} %bitcast.54), calls=%async_computation.2 | async-start | bytes 7340032 | tf_op jit(solution)/shard_map/all_to_all | solution.py:65
  296.2 5.0 %copy-start.1 = (bf16[128,1792]{1,0:T(8,128)(2,1)S(1)}, bf16[128,1792]{1,0:T(8,128)(2,1)}, u32[]{:S(2)}) copy-start(bf16[128,1792]{1,0:T(8,128)(2,1)} %param.11) | copy-start | bytes 1376260
Sparse Core Ops, SparseCore 0:
  22.5 117.0 all-gather.1
